TPU v7x, 32 devices: a whole 2x2x4 slice. The times are simulated.
32 devices in a mesh: sta: 16 (over z, x, core), strike: 2 (over y).
Axes of the slice: x: 2, y: 2, z: 4, core: 2. Of those that a mesh axis runs over, the one named last changes fastest.
Arguments:
- data: float32 [128, 512], P('sta'), may hold values from -6 to 6
- model: float32 [64, 64, 128], P(None, 'strike'), may hold values from -6 to 6
- green: bfloat16 [16, 2, 96, 128, 128], P('sta', 'strike'), may hold values from -0.03125 to 0.03125
- block_ids: int32 [16, 2, 96], P('sta', 'strike'), may hold values from -1 to 1023, as said below
Outputs:
- residual: float32 [128, 512], P('sta')
- updated: float32 [64, 64, 128], P(None, 'strike')
Inputs may be any that keep to these rules, and one draw needn't show every extreme that they name: In each block_ids[g, h] the ids that are not -1 are distinct and stand in the first slots; every pair uses at least a third of its 96 slots, and in every draw some pair uses all 96.
All inputs are finite; a program needn't handle non-finite values.
Results may differ from a plain program's by a relative error of at most 0.0023.
Values sent between devices are 32-bit elements; how exact they have to be, the bound alone decides.
A program may use at most 64 MiB of HBM per device.

v0:
```python
import jax
import jax.numpy as jnp
from jax import lax
from jax.sharding import PartitionSpec as P

SWEEPS = 4
NU_DIFF = 0.1
STEP_LEN = 4.0


def extended(block, sides, width):
    for axis, dim in sides:
        count = lax.axis_size(axis)
        forward = [(i, i + 1) for i in range(count - 1)]
        backward = [(target, source) for source, target in forward]
        low = lax.ppermute(
            lax.slice_in_dim(block, block.shape[dim] - width, None, axis=dim), axis, forward
        )
        high = lax.ppermute(lax.slice_in_dim(block, 0, width, axis=dim), axis, backward)
        block = jnp.concatenate([low, block, high], axis=dim)
    return block


def shear_add(series):
    count_rows, windows, length = series.shape
    padded = jnp.pad(series, ((0, 0), (0, 0), (0, windows)))
    flattened = padded.reshape(count_rows, windows * (length + windows))[
        :, : windows * (length + windows - 1)
    ]
    sheared = flattened.reshape(count_rows, windows, length + windows - 1)
    return jnp.sum(sheared[:, :, :length], axis=1)


def shear_take(residual, windows):
    count_rows, length = residual.shape
    padded = jnp.pad(residual, ((0, 0), (0, windows)))
    repeated = jnp.broadcast_to(padded[:, None, :], (count_rows, windows, length + windows))
    repeated = repeated.reshape(count_rows, windows * (length + windows))
    repeated = jnp.pad(repeated, ((0, 0), (0, windows)))
    return repeated.reshape(count_rows, windows, length + windows + 1)[:, :, :length]


def laplace_step(padded, field):
    laplace = (
        padded[:, 2:, 1:-1]
        + padded[:, :-2, 1:-1]
        + padded[:, 1:-1, 2:]
        + padded[:, 1:-1, :-2]
        - 4.0 * field
    )
    return field + NU_DIFF * laplace


def local(data, model, green, block_ids):
    sta_rows, samples = data.shape
    windows, strike_rows, dip_cells = model.shape
    block = green.shape[-1]
    time_blocks = samples // block
    row_count = sta_rows * time_blocks
    blocks = green.reshape(green.shape[2:])
    slot_ids = block_ids.reshape(-1)
    usable = slot_ids >= 0
    safe_ids = jnp.where(usable, slot_ids, 0)
    row_block = safe_ids // strike_rows
    col_block = safe_ids % strike_rows
    row_target = jnp.where(usable, row_block, row_count)
    col_target = jnp.where(usable, col_block, strike_rows)
    model_bf = model.astype(jnp.bfloat16)
    columns = jnp.take(model_bf, col_block, axis=1)
    products = jnp.einsum("cts,wcs->cwt", blocks, columns, preferred_element_type=jnp.float32)
    gathered = jax.ops.segment_sum(products, row_target, num_segments=row_count)
    series = (
        gathered.reshape(sta_rows, time_blocks, windows, block)
        .transpose(0, 2, 1, 3)
        .reshape(sta_rows, windows, samples)
    )
    partial_synth = shear_add(series)
    residual = lax.psum(partial_synth, "strike") - data
    resid_bf = residual.astype(jnp.bfloat16)
    shifted = shear_take(resid_bf, windows)
    row_blocks = (
        shifted.reshape(sta_rows, windows, time_blocks, block)
        .transpose(0, 2, 1, 3)
        .reshape(row_count, windows, block)
    )
    res_rows = jnp.take(row_blocks, row_block, axis=0)
    slot_grads = jnp.einsum("cts,cwt->cws", blocks, res_rows, preferred_element_type=jnp.float32)
    per_patch = jax.ops.segment_sum(slot_grads, col_target, num_segments=strike_rows)
    partial_grad = per_patch.transpose(1, 0, 2)
    field = lax.psum(partial_grad, "sta")
    for sweep in range(SWEEPS):
        padded = extended(field, (("strike", 1),), 1)
        padded = jnp.pad(padded, ((0, 0), (0, 0), (1, 1)))
        field = laplace_step(padded, field)
    updated = model - STEP_LEN * field
    return (residual, updated)


def solution(mesh):
    in_specs = (
        P("sta", None),
        P(None, "strike", None),
        P("sta", "strike", None, None, None),
        P("sta", "strike", None),
    )
    out_specs = (P("sta", None), P(None, "strike", None))
    return jax.shard_map(local, mesh=mesh, in_specs=in_specs, out_specs=out_specs, check_vma=False)
```

profile of v0, /device:TPU:0, one launch (start us, length us, event | category | flops | bytes accessed | tf_op | source)
XLA Modules:
  0.0 228.4 jit_solution(13629013439439119440)
XLA Ops:
  7.2 0.0 copy-start
  7.2 0.0 all-reduce.9.cloned.1.call-start
  7.2 0.8 fusion.33
  8.0 0.8 compare_and_fusion
  8.8 0.7 fusion.31
  9.5 2.6 %copy.16 = bf16[64,32,128]{2,0,1:T(8,128)(2,1)} copy(f32[64,32,128]{2,1,0:T(8,128)} %param.5) | data formatting | bytes 1572864 | tf_op args[1]
  12.1 3.0 %gather_fusion = bf16[96,64,128]{2,1,0:T(8,128)(2,1)} fusion(bf16[64,32,128]{2,0,1:T(8,128)(2,1)} %copy.16, s32[1024]{0:T(1024)S(1)} %pad_clamp_fusion.1), kind=kCustom, calls=%fused_computation | custom fusion | bytes 3146112 | tf_op jit(solution)/shard_map/jit(_take)/gather | solution.py:69
  15.1 0.0 copy-done
  15.1 5.3 %fusion.2 = f32[96,64,128]{2,1,0:T(8,128)} fusion(bf16[1,1,96,128,128]{4,3,2,1,0:T(8,128)(2,1)S(1)} %copy-done, bf16[96,64,128]{2,1,0:T(8,128)(2,1)} %gather_fusion, pred[96]{0:T(512)(128)(4,1)S(1)} %compare_and_fusion.1), kind=kOutput, calls=%fused_computation.8 | convolution fusion | flops 202113024 | bytes 7864416 | tf_op jit(solution)/shard_map/cts,wcs->cwt/dot_general | solution.py:70
  20.4 1.1 broadcast.280.clone
  21.5 14.6 %scatter_fusion = f32[32,64,128]{2,1,0:T(8,128)} fusion(f32[32,64,128]{2,1,0:T(8,128)} %broadcast.280.clone, s32[96]{0:T(128)S(1)} %get-tuple-element.25, f32[96,64,128]{2,1,0:T(8,128)} %fusion.2), kind=kCustom, calls=%fused_computation.2 | custom fusion | flops 786432 | bytes 9437568 | tf_op jit(solution)/shard_map/scatter-add | solution.py:71
  36.1 1.4 copy.17
  37.4 1.2 pad.25
  38.6 2.9 %reshape.180 = f32[8,36864]{1,0:T(8,128)} reshape(f32[8,64,576]{2,1,0:T(8,128)} %pad.25) | data formatting | bytes 2359296 | tf_op jit(solution)/shard_map/reshape | solution.py:27
  41.6 0.0 copy-start.3
  41.6 3.6 %reshape.181 = f32[8,64,575]{2,1,0:T(8,128)} reshape(f32[8,36800]{1,0:T(8,128)} %bitcast.46) | data formatting | bytes 2355200 | tf_op jit(solution)/shard_map/reshape | solution.py:30
  45.1 1.3 slice_reduce_fusion
  46.5 10.1 %psum.14 = f32[8,512]{1,0:T(8,128)S(1)} all-reduce(f32[8,512]{1,0:T(8,128)S(1)} %slice_reduce_fusion), channel_id=1, replica_groups=mesh['sta'=16,'strike'=2] {'strike'}, use_global_device_ids=true, to_apply=%region_2.3 | all-reduce | flops 4096 | bytes 32768 | tf_op jit(solution)/shard_map/psum | solution.py:78
  56.6 0.0 copy-done.3
  56.6 0.6 fusion.36
  57.2 0.9 broadcast_in_dim.35
  58.1 2.7 %reshape.182 = bf16[8,36864]{1,0:T(8,128)(2,1)} reshape(bf16[8,64,576]{2,1,0:T(8,128)(2,1)} %broadcast_in_dim.35) | data formatting | bytes 1179648 | tf_op jit(solution)/shard_map/reshape | solution.py:38
  60.8 1.9 pad.27
  62.7 3.3 %reshape.183 = bf16[8,64,577]{2,1,0:T(8,128)(2,1)} reshape(bf16[8,36928]{1,0:T(8,128)(2,1)} %pad.27) | data formatting | bytes 1181696 | tf_op jit(solution)/shard_map/reshape | solution.py:40
  66.0 1.1 fusion.41
  67.1 0.8 pad_maximum_fusion.8
  68.0 3.0 %gather_fusion.1 = bf16[96,64,128]{2,1,0:T(8,128)(2,1)} fusion(bf16[32,64,128]{2,1,0:T(8,128)(2,1)} %bitcast.45, s32[1024]{0:T(1024)S(1)} %pad_clamp_fusion), kind=kCustom, calls=%fused_computation.1 | custom fusion | bytes 3146112 | tf_op jit(solution)/shard_map/jit(_take)/gather | solution.py:86
  71.0 4.0 %fusion = f32[96,64,128]{2,1,0:T(8,128)} fusion(bf16[1,1,96,128,128]{4,3,2,1,0:T(8,128)(2,1)S(1)} %copy-done, bf16[96,64,128]{2,1,0:T(8,128)(2,1)} %gather_fusion.1, pred[96]{0:T(512)(128)(4,1)S(1)} %get-tuple-element.4), kind=kOutput, calls=%fused_computation.6 | convolution fusion | flops 202113024 | bytes 7864416 | tf_op jit(solution)/shard_map/cts,cwt->cws/dot_general | solution.py:87
  75.0 1.1 broadcast.280
  76.1 14.5 %scatter_fusion.1 = f32[32,64,128]{2,1,0:T(8,128)} fusion(f32[32,64,128]{2,1,0:T(8,128)} %broadcast.280, s32[96]{0:T(128)S(1)} %get-tuple-element.23, f32[96,64,128]{2,1,0:T(8,128)} %fusion), kind=kCustom, calls=%fused_computation.3 | custom fusion | flops 786432 | bytes 9437568 | tf_op jit(solution)/shard_map/scatter-add | solution.py:88
  90.7 0.0 all-reduce.9.cloned.1.call-update
  90.7 92.7 %all-reduce.9.cloned.1.call-done = f32[64,32,128]{2,0,1:T(8,128)} async-done(((f32[64,32,128]{2,0,1:T(8,128)}), f32[64,32,128]{2,0,1:T(8,128)}) %all-reduce.9.cloned.1.call-update) | async-done | bytes 1048592 | tf_op jit(solution)/shard_map/psum | solution.py:90
  183.4 0.0 copy-start.1
  183.4 0.9 fusion.40
  184.3 1.3 collective-permute-start
  185.6 4.5 %collective-permute-start.1 = (f32[64,1,128]{2,0,1:T(8,128)S(1)}, f32[64,1,128]{2,0,1:T(8,128)S(1)}, u32[]{:S(2)}, u32[]{:S(2)}) collective-permute-start(f32[64,1,128]{2,0,1:T(8,128)S(1)} %get-tuple-element.17), channel_id=1, source_target_pairs={{0,1},{2,3},{4,5},{6,7},{8,9},{10,11},{12,13},{14,15},{16,17},{18,... | collective-permute-start | bytes 98312 | tf_op jit(solution)/shard_map/ppermute | solution.py:16
  190.1 0.0 collective-permute-done
  190.1 1.6 collective-permute-done.1
  191.7 1.9 select_maximum_fusion.6
  193.6 0.0 copy-done.1
  193.6 0.4 fusion.26
  194.0 1.3 collective-permute-start.2
  195.3 4.5 %collective-permute-start.3 = (f32[64,1,128]{2,0,1:T(8,128)S(1)}, f32[64,1,128]{2,0,1:T(8,128)S(1)}, u32[]{:S(2)}, u32[]{:S(2)}) collective-permute-start(f32[64,1,128]{2,0,1:T(8,128)S(1)} %get-tuple-element.15), channel_id=1, source_target_pairs={{0,1},{2,3},{4,5},{6,7},{8,9},{10,11},{12,13},{14,15},{16,17},{18,... | collective-permute-start | bytes 98312 | tf_op jit(solution)/shard_map/ppermute | solution.py:16
  199.8 0.0 collective-permute-done.2
  199.8 1.6 collective-permute-done.3
  201.4 0.6 select_maximum_fusion.4
  202.0 0.4 fusion.22
  202.4 1.3 collective-permute-start.4
  203.7 4.7 %collective-permute-start.5 = (f32[64,1,128]{2,0,1:T(8,128)S(1)}, f32[64,1,128]{2,0,1:T(8,128)S(1)}, u32[]{:S(2)}, u32[]{:S(2)}) collective-permute-start(f32[64,1,128]{2,0,1:T(8,128)S(1)} %get-tuple-element.13), channel_id=1, source_target_pairs={{0,1},{2,3},{4,5},{6,7},{8,9},{10,11},{12,13},{14,15},{16,17},{18,... | collective-permute-start | bytes 98312 | tf_op jit(solution)/shard_map/ppermute | solution.py:16
  208.5 0.0 collective-permute-done.4
  208.5 1.4 collective-permute-done.5
  209.9 0.6 select_maximum_fusion.2
  210.5 0.4 fusion.18
  210.9 0.0 copy-start.2
  210.9 1.4 collective-permute-start.6
  212.3 4.5 %collective-permute-start.7 = (f32[64,1,128]{2,0,1:T(8,128)S(1)}, f32[64,1,128]{2,0,1:T(8,128)S(1)}, u32[]{:S(2)}, u32[]{:S(2)}) collective-permute-start(f32[64,1,128]{2,0,1:T(8,128)S(1)} %get-tuple-element.11), channel_id=1, source_target_pairs={{0,1},{2,3},{4,5},{6,7},{8,9},{10,11},{12,13},{14,15},{16,17},{18,... | collective-permute-start | bytes 98312 | tf_op jit(solution)/shard_map/ppermute | solution.py:16
  216.9 0.0 collective-permute-done.6
  216.9 1.6 collective-permute-done.7
  218.5 0.6 select_maximum_fusion
  219.1 0.0 copy-done.2
  219.1 0.9 fusion.14
  220.0 1.6 copy.11
  (7 shorter events, 0.0 us)
Async XLA Ops:
  7.2 8.0 %copy-start = (bf16[1,1,96,128,128]{4,3,2,1,0:T(8,128)(2,1)S(1)}, bf16[1,1,96,128,128]{4,3,2,1,0:T(8,128)(2,1)}, u32[]{:S(2)}) copy-start(bf16[1,1,96,128,128]{4,3,2,1,0:T(8,128)(2,1)} %param.6) | copy-start | bytes 9437188
  7.2 176.2 %all-reduce.9.cloned.1.call-start = ((), (), s32[]{:S(2)}) async-start(), calls=%async_computation | async-start | bytes 2097152 | tf_op jit(solution)/shard_map/psum | solution.py:90
  41.6 15.1 %copy-start.3 = (f32[8,512]{1,0:T(8,128)S(1)}, f32[8,512]{1,0:T(8,128)}, u32[]{:S(2)}) copy-start(f32[8,512]{1,0:T(8,128)} %param.4) | copy-start | bytes 49156
  183.4 10.2 %copy-start.1 = (f32[64,32,128]{2,0,1:T(8,128)S(1)}, f32[64,32,128]{2,0,1:T(8,128)}, u32[]{:S(2)}) copy-start(f32[64,32,128]{2,0,1:T(8,128)} %all-reduce.9.cloned.1.call-done) | copy-start | bytes 3145732
  184.3 5.8 %collective-permute-start = (f32[64,1,128]{2,0,1:T(8,128)S(1)}, f32[64,1,128]{2,0,1:T(8,128)S(1)}, u32[]{:S(2)}, u32[]{:S(2)}) collective-permute-start(f32[64,1,128]{2,0,1:T(8,128)S(1)} %get-tuple-element.18), channel_id=1, source_target_pairs={{1,0},{3,2},{5,4},{7,6},{9,8},{11,10},{13,12},{15,14},{17,16},{19,... | collective-permute-start | bytes 98312 | tf_op jit(solution)/shard_map/ppermute | solution.py:19
  185.6 6.1 %collective-permute-start.1 = (f32[64,1,128]{2,0,1:T(8,128)S(1)}, f32[64,1,128]{2,0,1:T(8,128)S(1)}, u32[]{:S(2)}, u32[]{:S(2)}) collective-permute-start(f32[64,1,128]{2,0,1:T(8,128)S(1)} %get-tuple-element.17), channel_id=1, source_target_pairs={{0,1},{2,3},{4,5},{6,7},{8,9},{10,11},{12,13},{14,15},{16,17},{18,... | collective-permute-start | bytes 98312 | tf_op jit(solution)/shard_map/ppermute | solution.py:16
  194.0 5.9 %collective-permute-start.2 = (f32[64,1,128]{2,0,1:T(8,128)S(1)}, f32[64,1,128]{2,0,1:T(8,128)S(1)}, u32[]{:S(2)}, u32[]{:S(2)}) collective-permute-start(f32[64,1,128]{2,0,1:T(8,128)S(1)} %get-tuple-element.16), channel_id=1, source_target_pairs={{1,0},{3,2},{5,4},{7,6},{9,8},{11,10},{13,12},{15,14},{17,16},{19,... | collective-permute-start | bytes 98312 | tf_op jit(solution)/shard_map/ppermute | solution.py:19
  195.3 6.1 %collective-permute-start.3 = (f32[64,1,128]{2,0,1:T(8,128)S(1)}, f32[64,1,128]{2,0,1:T(8,128)S(1)}, u32[]{:S(2)}, u32[]{:S(2)}) collective-permute-start(f32[64,1,128]{2,0,1:T(8,128)S(1)} %get-tuple-element.15), channel_id=1, source_target_pairs={{0,1},{2,3},{4,5},{6,7},{8,9},{10,11},{12,13},{14,15},{16,17},{18,... | collective-permute-start | bytes 98312 | tf_op jit(solution)/shard_map/ppermute | solution.py:16
  202.4 6.0 %collective-permute-start.4 = (f32[64,1,128]{2,0,1:T(8,128)S(1)}, f32[64,1,128]{2,0,1:T(8,128)S(1)}, u32[]{:S(2)}, u32[]{:S(2)}) collective-permute-start(f32[64,1,128]{2,0,1:T(8,128)S(1)} %get-tuple-element.14), channel_id=1, source_target_pairs={{1,0},{3,2},{5,4},{7,6},{9,8},{11,10},{13,12},{15,14},{17,16},{19,... | collective-permute-start | bytes 98312 | tf_op jit(solution)/shard_map/ppermute | solution.py:19
  203.7 6.1 %collective-permute-start.5 = (f32[64,1,128]{2,0,1:T(8,128)S(1)}, f32[64,1,128]{2,0,1:T(8,128)S(1)}, u32[]{:S(2)}, u32[]{:S(2)}) collective-permute-start(f32[64,1,128]{2,0,1:T(8,128)S(1)} %get-tuple-element.13), channel_id=1, source_target_pairs={{0,1},{2,3},{4,5},{6,7},{8,9},{10,11},{12,13},{14,15},{16,17},{18,... | collective-permute-start | bytes 98312 | tf_op jit(solution)/shard_map/ppermute | solution.py:16
  210.9 8.2 %copy-start.2 = (f32[64,32,128]{2,1,0:T(8,128)S(1)}, f32[64,32,128]{2,1,0:T(8,128)}, u32[]{:S(2)}) copy-start(f32[64,32,128]{2,1,0:T(8,128)} %param.5) | copy-start | bytes 3145732
  210.9 6.0 %collective-permute-start.6 = (f32[64,1,128]{2,0,1:T(8,128)S(1)}, f32[64,1,128]{2,0,1:T(8,128)S(1)}, u32[]{:S(2)}, u32[]{:S(2)}) collective-permute-start(f32[64,1,128]{2,0,1:T(8,128)S(1)} %get-tuple-element.12), channel_id=1, source_target_pairs={{1,0},{3,2},{5,4},{7,6},{9,8},{11,10},{13,12},{15,14},{17,16},{19,... | collective-permute-start | bytes 98312 | tf_op jit(solution)/shard_map/ppermute | solution.py:19
  212.3 6.1 %collective-permute-start.7 = (f32[64,1,128]{2,0,1:T(8,128)S(1)}, f32[64,1,128]{2,0,1:T(8,128)S(1)}, u32[]{:S(2)}, u32[]{:S(2)}) collective-permute-start(f32[64,1,128]{2,0,1:T(8,128)S(1)} %get-tuple-element.11), channel_id=1, source_target_pairs={{0,1},{2,3},{4,5},{6,7},{8,9},{10,11},{12,13},{14,15},{16,17},{18,... | collective-permute-start | bytes 98312 | tf_op jit(solution)/shard_map/ppermute | solution.py:16
Sparse Core Ops, SparseCore 0:
  90.8 92.5 all-reduce.8
where the time goes:
time: 230 us; the launch traced here: 228 us
  waiting for transfers between devices  98.8 us (43%)
  other arithmetic  39.9 us (17%)
  local copies, waits for them, and re-layouts  32.3 us (14%)
  starting transfers between devices  23.7 us (10%)
  between operations  14.3 us (6%)
  blocking collectives  10.1 us (4%)
  matrix products  9.33 us (4%)
    psum x1, waiting for transfers between devices, local(): field = lax.psum(partial_grad, 'sta')  92.7 us
    ppermute x4, starting transfers between devices, extended(): lax.ppermute(lax.slice_in_dim(block, block.shape[dim] - width, None, axis...  18.4 us
    scatter-add x1, other arithmetic, local(): gathered = jax.ops.segment_sum(products, row_target, num_segments=row_count)  14.6 us
    scatter-add x1, other arithmetic, local(): jax.ops.segment_sum(slot_grads, col_target, num_segments=strike_rows)  14.5 us
    psum x1, blocking collectives, local(): residual = lax.psum(partial_synth, 'strike') - data  10.1 us
    ppermute x4, waiting for transfers between devices, extended(): lax.ppermute(lax.slice_in_dim(block, block.shape[dim] - width, None, axis...  6.09 us
    ppermute x4, starting transfers between devices, extended(): lax.ppermute(lax.slice_in_dim(block, 0, width, axis=dim), axis, backward)  5.29 us
    dot_general x1, matrix products, local(): jnp.einsum('cts,wcs->cwt', blocks, columns, preferred_element_type=jnp.fl...  5.28 us
  transfers between devices with their start and end apart: 9, of which 5 were waited for; matrix products, arithmetic and copies ran while one was open for 0% of the time, Pallas kernels for 0%

commit v1 on v0

--- a/solution.py
+++ b/solution.py
@@ -6,6 +6,12 @@
 SWEEPS = 4
 NU_DIFF = 0.1
 STEP_LEN = 4.0
+
+
+def render_the_face(mat):
+    y2 = jax.lax.all_gather(mat, "sta")
+    h_now = jnp.sum(y2, 0)
+    return h_now
 
 
 def extended(block, sides, width):
@@ -87,7 +93,7 @@
     slot_grads = jnp.einsum("cts,cwt->cws", blocks, res_rows, preferred_element_type=jnp.float32)
     per_patch = jax.ops.segment_sum(slot_grads, col_target, num_segments=strike_rows)
     partial_grad = per_patch.transpose(1, 0, 2)
-    field = lax.psum(partial_grad, "sta")
+    field = render_the_face(partial_grad)
     for sweep in range(SWEEPS):
         padded = extended(field, (("strike", 1),), 1)
         padded = jnp.pad(padded, ((0, 0), (0, 0), (1, 1)))

time: 230 us -> 271 us (1.18)
  waiting for transfers between devices: 98.8 us -> 132 us
  other arithmetic: 39.9 us -> 48.8 us
    all_gather x0 -> x1, waiting for transfers between devices: none -> 126 us  [render_the_face(): y2 = jax.lax.all_gather(mat, 'sta')]
    psum x1 -> x0, waiting for transfers between devices: 92.7 us -> none  [local(): field = lax.psum(partial_grad, 'sta')]
    reduce_sum x0 -> x1, other arithmetic: none -> 8.92 us  [render_the_face(): h_now = jnp.sum(y2, 0)]
where the time goes in v1:
time: 271 us; the launch traced here: 270 us
  waiting for transfers between devices  132 us (49%)
  other arithmetic  48.8 us (18%)
  local copies, waits for them, and re-layouts  32.3 us (12%)
  starting transfers between devices  23.5 us (9%)
  between operations  14.3 us (5%)
  blocking collectives  10.1 us (4%)
  matrix products  9.33 us (3%)
    all_gather x1, waiting for transfers between devices, render_the_face(): y2 = jax.lax.all_gather(mat, 'sta')  126 us
    ppermute x4, starting transfers between devices, extended(): lax.ppermute(lax.slice_in_dim(block, block.shape[dim] - width, None, axis...  18.2 us
    scatter-add x1, other arithmetic, local(): gathered = jax.ops.segment_sum(products, row_target, num_segments=row_count)  14.5 us
    scatter-add x1, other arithmetic, local(): jax.ops.segment_sum(slot_grads, col_target, num_segments=strike_rows)  14.5 us
    psum x1, blocking collectives, local(): residual = lax.psum(partial_synth, 'strike') - data  10.1 us
    reduce_sum x1, other arithmetic, render_the_face(): h_now = jnp.sum(y2, 0)  8.92 us
    ppermute x4, waiting for transfers between devices, extended(): lax.ppermute(lax.slice_in_dim(block, block.shape[dim] - width, None, axis...  6.27 us
  transfers between devices with their start and end apart: 9, of which 5 were waited for; matrix products, arithmetic and copies ran while one was open for 0% of the time, Pallas kernels for 0%

profile of v1, /device:TPU:0, one launch (start us, length us, event | category | flops | bytes accessed | tf_op | source)
XLA Modules:
  0.0 270.1 jit_solution(14735303442725386322)
XLA Ops:
  7.2 0.0 copy-start
  7.2 0.0 all-gather.3.cloned.1.call-start
  7.2 0.8 fusion.33
  8.0 0.8 compare_and_fusion
  8.8 2.6 copy.19
  11.4 0.7 fusion.31
  12.1 3.0 %gather_fusion = bf16[96,64,128]{2,1,0:T(8,128)(2,1)} fusion(bf16[64,32,128]{2,0,1:T(8,128)(2,1)} %copy.19, s32[1024]{0:T(1024)S(1)} %pad_clamp_fusion.1), kind=kCustom, calls=%fused_computation | custom fusion | bytes 3146112 | tf_op jit(solution)/shard_map/jit(_take)/gather | solution.py:75
  15.1 0.0 copy-done
  15.1 5.3 %fusion.2 = f32[96,64,128]{2,1,0:T(8,128)} fusion(bf16[1,1,96,128,128]{4,3,2,1,0:T(8,128)(2,1)S(1)} %copy-done, bf16[96,64,128]{2,1,0:T(8,128)(2,1)} %gather_fusion, pred[96]{0:T(512)(128)(4,1)S(1)} %compare_and_fusion.1), kind=kOutput, calls=%fused_computation.8 | convolution fusion | flops 202113024 | bytes 7864416 | tf_op jit(solution)/shard_map/cts,wcs->cwt/dot_general | solution.py:76
  20.4 1.1 broadcast.280.clone
  21.5 14.5 %scatter_fusion = f32[32,64,128]{2,1,0:T(8,128)} fusion(f32[32,64,128]{2,1,0:T(8,128)} %broadcast.280.clone, s32[96]{0:T(128)S(1)} %get-tuple-element.25, f32[96,64,128]{2,1,0:T(8,128)} %fusion.2), kind=kCustom, calls=%fused_computation.2 | custom fusion | flops 786432 | bytes 9437568 | tf_op jit(solution)/shard_map/scatter-add | solution.py:77
  36.0 1.4 copy.20
  37.4 1.2 pad.25
  38.6 2.9 %reshape.180 = f32[8,36864]{1,0:T(8,128)} reshape(f32[8,64,576]{2,1,0:T(8,128)} %pad.25) | data formatting | bytes 2359296 | tf_op jit(solution)/shard_map/reshape | solution.py:33
  41.5 0.0 copy-start.3
  41.5 3.6 %reshape.181 = f32[8,64,575]{2,1,0:T(8,128)} reshape(f32[8,36800]{1,0:T(8,128)} %bitcast.48) | data formatting | bytes 2355200 | tf_op jit(solution)/shard_map/reshape | solution.py:36
  45.1 1.3 slice_reduce_fusion
  46.5 10.1 %psum.7 = f32[8,512]{1,0:T(8,128)S(1)} all-reduce(f32[8,512]{1,0:T(8,128)S(1)} %slice_reduce_fusion), channel_id=1, replica_groups=mesh['sta'=16,'strike'=2] {'strike'}, use_global_device_ids=true, to_apply=%region_2.3 | all-reduce | flops 4096 | bytes 32768 | tf_op jit(solution)/shard_map/psum | solution.py:84
  56.6 0.0 copy-done.3
  56.6 0.6 fusion.36
  57.2 0.9 broadcast_in_dim.35
  58.1 2.7 reshape.182
  60.8 1.9 pad.27
  62.7 3.3 %reshape.183 = bf16[8,64,577]{2,1,0:T(8,128)(2,1)} reshape(bf16[8,36928]{1,0:T(8,128)(2,1)} %pad.27) | data formatting | bytes 1181696 | tf_op jit(solution)/shard_map/reshape | solution.py:46
  66.0 1.1 fusion.41
  67.1 0.8 pad_maximum_fusion.8
  68.0 3.0 %gather_fusion.1 = bf16[96,64,128]{2,1,0:T(8,128)(2,1)} fusion(bf16[32,64,128]{2,1,0:T(8,128)(2,1)} %bitcast.47, s32[1024]{0:T(1024)S(1)} %pad_clamp_fusion), kind=kCustom, calls=%fused_computation.1 | custom fusion | bytes 3146112 | tf_op jit(solution)/shard_map/jit(_take)/gather | solution.py:92
  70.9 4.0 %fusion = f32[96,64,128]{2,1,0:T(8,128)} fusion(bf16[1,1,96,128,128]{4,3,2,1,0:T(8,128)(2,1)S(1)} %copy-done, bf16[96,64,128]{2,1,0:T(8,128)(2,1)} %gather_fusion.1, pred[96]{0:T(512)(128)(4,1)S(1)} %get-tuple-element.4), kind=kOutput, calls=%fused_computation.6 | convolution fusion | flops 202113024 | bytes 7864416 | tf_op jit(solution)/shard_map/cts,cwt->cws/dot_general | solution.py:93
  75.0 1.1 broadcast.280
  76.1 14.5 %scatter_fusion.1 = f32[32,64,128]{2,1,0:T(8,128)} fusion(f32[32,64,128]{2,1,0:T(8,128)} %broadcast.280, s32[96]{0:T(128)S(1)} %get-tuple-element.23, f32[96,64,128]{2,1,0:T(8,128)} %fusion), kind=kCustom, calls=%fused_computation.3 | custom fusion | flops 786432 | bytes 9437568 | tf_op jit(solution)/shard_map/scatter-add | solution.py:94
  90.6 0.0 all-gather.3.cloned.1.call-update
  90.7 125.5 %all-gather.3.cloned.1.call-done = f32[1024,32,128]{2,0,1:T(8,128)} async-done(((f32[64,32,128]{2,0,1:T(8,128)}), f32[1024,32,128]{2,0,1:T(8,128)}) %all-gather.3.cloned.1.call-update) | async-done | bytes 16777232 | tf_op jit(solution)/shard_map/all_gather | solution.py:12
  216.2 8.9 %reduce_sum.19 = f32[64,32,128]{2,0,1:T(8,128)} reduce(f32[16,64,32,128]{3,1,0,2:T(8,128)} %bitcast.46, f32[]{:T(128)} %constant.56.clone.1), dimensions={0}, to_apply=%region_4.5 | reduce | flops 3932160 | bytes 17825796 | tf_op jit(solution)/shard_map/reduce_sum | solution.py:13
  225.1 0.0 copy-start.1
  225.1 0.9 fusion.40
  226.0 1.3 collective-permute-start
  227.3 4.5 %collective-permute-start.1 = (f32[64,1,128]{2,0,1:T(8,128)S(1)}, f32[64,1,128]{2,0,1:T(8,128)S(1)}, u32[]{:S(2)}, u32[]{:S(2)}) collective-permute-start(f32[64,1,128]{2,0,1:T(8,128)S(1)} %get-tuple-element.17), channel_id=1, source_target_pairs={{0,1},{2,3},{4,5},{6,7},{8,9},{10,11},{12,13},{14,15},{16,17},{18,... | collective-permute-start | bytes 98312 | tf_op jit(solution)/shard_map/ppermute | solution.py:22
  231.8 0.0 collective-permute-done
  231.8 1.6 collective-permute-done.1
  233.4 1.9 select_maximum_fusion.6
  235.3 0.0 copy-done.1
  235.3 0.4 fusion.26
  235.6 1.3 collective-permute-start.2
  236.9 4.5 %collective-permute-start.3 = (f32[64,1,128]{2,0,1:T(8,128)S(1)}, f32[64,1,128]{2,0,1:T(8,128)S(1)}, u32[]{:S(2)}, u32[]{:S(2)}) collective-permute-start(f32[64,1,128]{2,0,1:T(8,128)S(1)} %get-tuple-element.15), channel_id=1, source_target_pairs={{0,1},{2,3},{4,5},{6,7},{8,9},{10,11},{12,13},{14,15},{16,17},{18,... | collective-permute-start | bytes 98312 | tf_op jit(solution)/shard_map/ppermute | solution.py:22
  241.5 0.0 collective-permute-done.2
  241.5 1.6 collective-permute-done.3
  243.1 0.6 select_maximum_fusion.4
  243.7 0.4 fusion.22
  244.1 1.3 collective-permute-start.4
  245.4 4.5 %collective-permute-start.5 = (f32[64,1,128]{2,0,1:T(8,128)S(1)}, f32[64,1,128]{2,0,1:T(8,128)S(1)}, u32[]{:S(2)}, u32[]{:S(2)}) collective-permute-start(f32[64,1,128]{2,0,1:T(8,128)S(1)} %get-tuple-element.13), channel_id=1, source_target_pairs={{0,1},{2,3},{4,5},{6,7},{8,9},{10,11},{12,13},{14,15},{16,17},{18,... | collective-permute-start | bytes 98312 | tf_op jit(solution)/shard_map/ppermute | solution.py:22
  250.0 0.0 collective-permute-done.4
  250.0 1.6 collective-permute-done.5
  251.5 0.6 select_maximum_fusion.2
  252.2 0.4 fusion.18
  252.6 0.0 copy-start.2
  252.6 1.4 collective-permute-start.6
  254.1 4.5 %collective-permute-start.7 = (f32[64,1,128]{2,0,1:T(8,128)S(1)}, f32[64,1,128]{2,0,1:T(8,128)S(1)}, u32[]{:S(2)}, u32[]{:S(2)}) collective-permute-start(f32[64,1,128]{2,0,1:T(8,128)S(1)} %get-tuple-element.11), channel_id=1, source_target_pairs={{0,1},{2,3},{4,5},{6,7},{8,9},{10,11},{12,13},{14,15},{16,17},{18,... | collective-permute-start | bytes 98312 | tf_op jit(solution)/shard_map/ppermute | solution.py:22
  258.6 0.0 collective-permute-done.6
  258.6 1.6 collective-permute-done.7
  260.2 0.6 select_maximum_fusion
  260.8 0.0 copy-done.2
  260.8 0.8 fusion.14
  261.7 1.6 copy.14
  (7 shorter events, 0.0 us)
Async XLA Ops:
  7.2 8.0 %copy-start = (bf16[1,1,96,128,128]{4,3,2,1,0:T(8,128)(2,1)S(1)}, bf16[1,1,96,128,128]{4,3,2,1,0:T(8,128)(2,1)}, u32[]{:S(2)}) copy-start(bf16[1,1,96,128,128]{4,3,2,1,0:T(8,128)(2,1)} %param.6) | copy-start | bytes 9437188
  7.2 209.0 %all-gather.3.cloned.1.call-start = ((), (), s32[]{:S(2)}) async-start(), calls=%async_computation | async-start | bytes 17825792 | tf_op jit(solution)/shard_map/all_gather | solution.py:12
  41.5 15.1 %copy-start.3 = (f32[8,512]{1,0:T(8,128)S(1)}, f32[8,512]{1,0:T(8,128)}, u32[]{:S(2)}) copy-start(f32[8,512]{1,0:T(8,128)} %param.4) | copy-start | bytes 49156
  225.1 10.2 %copy-start.1 = (f32[64,32,128]{2,0,1:T(8,128)S(1)}, f32[64,32,128]{2,0,1:T(8,128)}, u32[]{:S(2)}) copy-start(f32[64,32,128]{2,0,1:T(8,128)} %reduce_sum.19) | copy-start | bytes 3145732
  226.0 5.8 %collective-permute-start = (f32[64,1,128]{2,0,1:T(8,128)S(1)}, f32[64,1,128]{2,0,1:T(8,128)S(1)}, u32[]{:S(2)}, u32[]{:S(2)}) collective-permute-start(f32[64,1,128]{2,0,1:T(8,128)S(1)} %get-tuple-element.18), channel_id=1, source_target_pairs={{1,0},{3,2},{5,4},{7,6},{9,8},{11,10},{13,12},{15,14},{17,16},{19,... | collective-permute-start | bytes 98312 | tf_op jit(solution)/shard_map/ppermute | solution.py:25
  227.3 6.1 %collective-permute-start.1 = (f32[64,1,128]{2,0,1:T(8,128)S(1)}, f32[64,1,128]{2,0,1:T(8,128)S(1)}, u32[]{:S(2)}, u32[]{:S(2)}) collective-permute-start(f32[64,1,128]{2,0,1:T(8,128)S(1)} %get-tuple-element.17), channel_id=1, source_target_pairs={{0,1},{2,3},{4,5},{6,7},{8,9},{10,11},{12,13},{14,15},{16,17},{18,... | collective-permute-start | bytes 98312 | tf_op jit(solution)/shard_map/ppermute | solution.py:22
  235.6 5.9 %collective-permute-start.2 = (f32[64,1,128]{2,0,1:T(8,128)S(1)}, f32[64,1,128]{2,0,1:T(8,128)S(1)}, u32[]{:S(2)}, u32[]{:S(2)}) collective-permute-start(f32[64,1,128]{2,0,1:T(8,128)S(1)} %get-tuple-element.16), channel_id=1, source_target_pairs={{1,0},{3,2},{5,4},{7,6},{9,8},{11,10},{13,12},{15,14},{17,16},{19,... | collective-permute-start | bytes 98312 | tf_op jit(solution)/shard_map/ppermute | solution.py:25
  236.9 6.1 %collective-permute-start.3 = (f32[64,1,128]{2,0,1:T(8,128)S(1)}, f32[64,1,128]{2,0,1:T(8,128)S(1)}, u32[]{:S(2)}, u32[]{:S(2)}) collective-permute-start(f32[64,1,128]{2,0,1:T(8,128)S(1)} %get-tuple-element.15), channel_id=1, source_target_pairs={{0,1},{2,3},{4,5},{6,7},{8,9},{10,11},{12,13},{14,15},{16,17},{18,... | collective-permute-start | bytes 98312 | tf_op jit(solution)/shard_map/ppermute | solution.py:22
  244.1 5.9 %collective-permute-start.4 = (f32[64,1,128]{2,0,1:T(8,128)S(1)}, f32[64,1,128]{2,0,1:T(8,128)S(1)}, u32[]{:S(2)}, u32[]{:S(2)}) collective-permute-start(f32[64,1,128]{2,0,1:T(8,128)S(1)} %get-tuple-element.14), channel_id=1, source_target_pairs={{1,0},{3,2},{5,4},{7,6},{9,8},{11,10},{13,12},{15,14},{17,16},{19,... | collective-permute-start | bytes 98312 | tf_op jit(solution)/shard_map/ppermute | solution.py:25
  245.4 6.1 %collective-permute-start.5 = (f32[64,1,128]{2,0,1:T(8,128)S(1)}, f32[64,1,128]{2,0,1:T(8,128)S(1)}, u32[]{:S(2)}, u32[]{:S(2)}) collective-permute-start(f32[64,1,128]{2,0,1:T(8,128)S(1)} %get-tuple-element.13), channel_id=1, source_target_pairs={{0,1},{2,3},{4,5},{6,7},{8,9},{10,11},{12,13},{14,15},{16,17},{18,... | collective-permute-start | bytes 98312 | tf_op jit(solution)/shard_map/ppermute | solution.py:22
  252.6 8.2 %copy-start.2 = (f32[64,32,128]{2,1,0:T(8,128)S(1)}, f32[64,32,128]{2,1,0:T(8,128)}, u32[]{:S(2)}) copy-start(f32[64,32,128]{2,1,0:T(8,128)} %param.5) | copy-start | bytes 3145732
  252.6 6.0 %collective-permute-start.6 = (f32[64,1,128]{2,0,1:T(8,128)S(1)}, f32[64,1,128]{2,0,1:T(8,128)S(1)}, u32[]{:S(2)}, u32[]{:S(2)}) collective-permute-start(f32[64,1,128]{2,0,1:T(8,128)S(1)} %get-tuple-element.12), channel_id=1, source_target_pairs={{1,0},{3,2},{5,4},{7,6},{9,8},{11,10},{13,12},{15,14},{17,16},{19,... | collective-permute-start | bytes 98312 | tf_op jit(solution)/shard_map/ppermute | solution.py:25
  254.1 6.1 %collective-permute-start.7 = (f32[64,1,128]{2,0,1:T(8,128)S(1)}, f32[64,1,128]{2,0,1:T(8,128)S(1)}, u32[]{:S(2)}, u32[]{:S(2)}) collective-permute-start(f32[64,1,128]{2,0,1:T(8,128)S(1)} %get-tuple-element.11), channel_id=1, source_target_pairs={{0,1},{2,3},{4,5},{6,7},{8,9},{10,11},{12,13},{14,15},{16,17},{18,... | collective-permute-start | bytes 98312 | tf_op jit(solution)/shard_map/ppermute | solution.py:22
Sparse Core Ops, SparseCore 0:
  90.8 125.3 all-gather.2
